TPU v7x, 512 devices: a whole 4x8x8 slice. The times are simulated.
512 devices in a mesh: frame: 32 (over z, x), tile: 16 (over y, core).
Axes of the slice: x: 4, y: 8, z: 8, core: 2. Of those that a mesh axis runs over, the one named last changes fastest.
Arguments:
- frames: bfloat16 [32, 3, 64, 256, 256], P('frame', None, None, 'tile'), may hold values from -6 to 6
- state_in: bfloat16 [32, 64, 256, 256], P('frame', None, 'tile'), may hold values from -6 to 6
- motion: int32 [3, 32, 3, 256], replicated, may hold values from -4 to 255, as said below
- merge_w: bfloat16 [64, 1152], replicated, may hold values from -0.1875 to 0.1875
- res_w: bfloat16 [1, 2, 64, 576], replicated, may hold values from -0.25 to 0.25
Outputs:
- states: bfloat16 [32, 3, 64, 256, 256], P('frame', None, None, 'tile')
Inputs may be any that keep to these rules, and one draw needn't show every extreme that they name: motion[0] names a source block of the same frame; blocks t * 16 to t * 16 + 15 form tile owner t. For each section, tick and owner, at most 2 of the owner's 16 destination blocks read blocks of any one owner, and exactly 2 read one owner. motion[1] and motion[2] lie in -4 to 4.
All inputs are finite; a program needn't handle non-finite values.
Results may differ from a plain program's by a relative error of at most 0.0095.
Values may be sent and summed in bfloat16 or wider, within the bound.
A program may use at most 64 MiB of HBM per device.

v0:
```python
import functools

import jax
import jax.numpy as jnp
from jax import lax
from jax.experimental import pallas as pl
from jax.experimental.pallas import tpu as pltpu
from jax.sharding import PartitionSpec as P

BW = 32
MESH = pl.DeviceIdType.MESH
F32, BF16 = jnp.float32, jnp.bfloat16
BATCHES = 4


def row_taps(halves, lane):
    low, high = halves
    down_low, down_high = pltpu.roll(low, BW, 1), pltpu.roll(high, BW, 1)
    up_low, up_high = pltpu.roll(low, 128 - BW, 1), pltpu.roll(high, 128 - BW, 1)
    first, last = lane < BW, lane >= 128 - BW
    zero = jnp.zeros_like(low)
    left = jnp.concatenate(
        [jnp.where(first, zero, down_low), low, jnp.where(last, up_high, up_low)], axis=0
    )
    right = jnp.concatenate(
        [jnp.where(first, down_low, down_high), high, jnp.where(last, zero, up_high)], axis=0
    )
    return jnp.concatenate([left.astype(BF16), right.astype(BF16)], axis=1)


def column_sum(product, width, col):
    halves = []
    for half in range(2):
        part = product[:, 128 * half : 128 * half + 128]
        before = jnp.where(col > 0, pltpu.roll(part[:width], 1, 1), 0.0)
        after = jnp.where(col < BW - 1, pltpu.roll(part[2 * width :], 127, 1), 0.0)
        halves.append(before + part[width : 2 * width] + after)
    return halves


def kernel(
    tiles, sections, ticks, motion_ref, first_ref, frames_ref, weight_ref, out_ref,
    moves, pieces, held_0, held_1, held_2, picked, arrived, part,
    moves_sem, one_send, one_recv, two_send, two_recv,
):
    held = (held_0, held_1, held_2)
    section = lax.axis_index("frame")
    owner = lax.axis_index("tile")
    ahead = lax.rem(section + 1, sections)
    behind = lax.rem(section + sections - 1, sections)
    per_owner = pieces.shape[2]
    width = out_ref.shape[2]
    span = per_owner // BATCHES

    moves_copy = pltpu.make_async_copy(motion_ref.at[:, section], moves, moves_sem)
    moves_copy.start()

    barrier = pltpu.get_barrier_semaphore()

    @pl.loop(1, tiles)
    def _(step):
        pl.semaphore_signal(
            barrier, inc=1, device_id={"tile": lax.rem(owner + step, tiles)}, device_id_type=MESH
        )

    @pl.loop(0, tiles)
    def _(step):
        pl.semaphore_signal(
            barrier, inc=1, device_id={"frame": behind, "tile": step}, device_id_type=MESH
        )

    pl.semaphore_wait(barrier, 2 * tiles - 1)

    def partner(step):
        turn = (step + 1) // 2 * (1 - 2 * lax.rem(step, 2))
        return lax.rem(owner + tiles // 2 + turn + tiles, tiles)

    def spread(source, target, send_sem, recv_sem):
        @pl.loop(0, tiles)
        def _(step):
            other = partner(step)

            @pl.when(other != owner)
            def _():
                pltpu.make_async_remote_copy(
                    src_ref=source(other), dst_ref=target, send_sem=send_sem, recv_sem=recv_sem,
                    device_id={"tile": other}, device_id_type=MESH,
                ).start()

            @pl.when(other == owner)
            def _():
                pltpu.make_async_copy(source(other), target, recv_sem).start()

    lane = lax.broadcasted_iota(jnp.int32, (width, 128), 1)
    col = lax.rem(lane, BW)
    pixels = 8 * BW
    place = lax.broadcasted_iota(jnp.int32, (1, pixels), 1)
    row_id = lax.broadcasted_iota(jnp.int32, (pixels, pixels), 0)

    spread(
        lambda other: first_ref.at[other], held[0].at[owner], one_send.at[0], one_recv.at[0]
    )

    for tick in range(ticks):
        def frame_part(block, carry, tick=tick):
            value = frames_ref[tick, block].astype(F32)
            part[block] = jnp.dot(
                weight_ref[0],
                row_taps((value[:, :128], value[:, 128:]), lane),
                preferred_element_type=F32,
            )
            return carry

        lax.fori_loop(0, per_owner, frame_part, 0)

        if tick == 0:
            moves_copy.wait()
        pltpu.make_async_copy(held[tick], held[tick], one_recv.at[tick]).wait()

        for batch in range(BATCHES):
            def pick(dest, carry, tick=tick, batch=batch):
                for local in range(span):
                    slot = batch * span + local
                    source = moves[0, tick, dest * per_owner + slot]
                    picked[tick, dest, slot] = held[tick][
                        source // per_owner, lax.rem(source, per_owner)
                    ]
                return carry

            lax.fori_loop(0, tiles, pick, 0)
            group = pl.ds(batch * span, span)
            spread(
                lambda other: picked.at[tick, other, group],
                arrived.at[tick, owner, group],
                two_send.at[tick, batch],
                two_recv.at[tick, batch],
            )

        for batch in range(BATCHES):
            group = pl.ds(batch * span, span)
            landed = arrived.at[tick, :, group]
            pltpu.make_async_copy(landed, landed, two_recv.at[tick, batch]).wait()

            def one_block(local, carry, tick=tick, batch=batch):
                block = batch * span + local
                down_by = moves[1, tick, owner * per_owner + block]
                right_by = moves[2, tick, owner * per_owner + block]
                row_at, col_at = place // BW + down_by, lax.rem(place, BW) + right_by
                inside = (row_at >= 0) & (row_at < 8) & (col_at >= 0) & (col_at < BW)
                wanted = jnp.where(inside, row_at * BW + col_at, -1)
                table = jnp.where(row_id == wanted, 1.0, 0.0).astype(BF16)
                value = jnp.concatenate(
                    [
                        jnp.concatenate(
                            [
                                arrived[tick, 2 * i + j, block].astype(F32)
                                for i in range(width // 8)
                            ],
                            axis=0,
                        )
                        for j in range(2)
                    ],
                    axis=1,
                ).astype(BF16)
                warped = jnp.dot(value, table, preferred_element_type=F32)
                product = part[block] + jnp.dot(
                    weight_ref[1],
                    row_taps((warped[:, :128], warped[:, 128:]), lane),
                    preferred_element_type=F32,
                )
                merged = [
                    jnp.where(half > 0, half, 0.1 * half).astype(BF16).astype(F32)
                    for half in column_sum(product, width, col)
                ]
                product = jnp.dot(
                    weight_ref[2], row_taps(merged, lane), preferred_element_type=F32
                )
                middle = [
                    jnp.maximum(half, 0.0).astype(BF16).astype(F32)
                    for half in column_sum(product, width, col)
                ]
                product = jnp.dot(
                    weight_ref[3], row_taps(middle, lane), preferred_element_type=F32
                )
                added = column_sum(product, width, col)
                for j in range(2):
                    hidden = merged[j] + added[j]
                    out_ref[tick, block, :, 128 * j : 128 * j + 128] = hidden.astype(BF16)
                    if tick + 1 < ticks:
                        for i in range(width // 8):
                            pieces[tick, 2 * i + j, block] = hidden[8 * i : 8 * i + 8].astype(BF16)
                return carry

            lax.fori_loop(0, span, one_block, 0)

            if tick + 1 < ticks:
                @pl.loop(0, tiles)
                def _(step, tick=tick, group=group):
                    other = partner(step)
                    pltpu.make_async_remote_copy(
                        src_ref=pieces.at[tick, other, group],
                        dst_ref=held[tick + 1].at[owner, group],
                        send_sem=one_send.at[tick + 1],
                        recv_sem=one_recv.at[tick + 1],
                        device_id={"frame": ahead, "tile": other},
                        device_id_type=MESH,
                    ).start()

    sent = first_ref.at[pl.ds(0, tiles - 1)]
    pltpu.make_async_copy(sent, sent, one_send.at[0]).wait()
    for tick in range(ticks):
        if tick + 1 < ticks:
            sent = pieces.at[tick]
            pltpu.make_async_copy(sent, sent, one_send.at[tick + 1]).wait()
        for batch in range(BATCHES):
            sent = picked.at[tick, pl.ds(0, tiles - 1), pl.ds(batch * span, span)]
            pltpu.make_async_copy(sent, sent, two_send.at[tick, batch]).wait()


def stacked_weight(weight):
    out_width, columns = weight.shape
    taps = weight.reshape(out_width, 3, 3, columns // 9)
    return jnp.transpose(taps, (2, 0, 1, 3))


def per_device(frames, state_in, motion, merge_w, res_w, tiles, sections):
    ticks, width, per_owner, pixels = frames.shape[1:]
    first = state_in[0].reshape(width // 8, 8, per_owner, 2, 128)
    first = jnp.transpose(first, (0, 3, 2, 1, 4)).reshape(tiles, per_owner, 8, 128)
    blocks = jnp.transpose(frames[0], (0, 2, 1, 3))
    merge = stacked_weight(merge_w)
    weight = jnp.stack(
        [
            merge[..., :width], merge[..., width:],
            stacked_weight(res_w[0, 0]), stacked_weight(res_w[0, 1]),
        ]
    ).reshape(4, 3 * width, 3 * width)
    vmem = pl.BlockSpec(memory_space=pltpu.VMEM)
    piece = (per_owner, 8, 128)
    out = pl.pallas_call(
        functools.partial(kernel, tiles, sections, ticks),
        out_shape=jax.ShapeDtypeStruct((ticks, per_owner, width, pixels), BF16),
        in_specs=[pl.BlockSpec(memory_space=pl.ANY), vmem, vmem, vmem],
        out_specs=vmem,
        scratch_shapes=[
            pltpu.SMEM((3, ticks, tiles * per_owner), jnp.int32),
            pltpu.VMEM((ticks - 1, tiles) + piece, BF16),
            pltpu.VMEM((tiles,) + piece, BF16),
            pltpu.VMEM((tiles,) + piece, BF16),
            pltpu.VMEM((tiles,) + piece, BF16),
            pltpu.VMEM((ticks, tiles) + piece, BF16),
            pltpu.VMEM((ticks, tiles) + piece, BF16),
            pltpu.VMEM((per_owner, 3 * width, pixels), F32),
            pltpu.SemaphoreType.DMA(()),
            pltpu.SemaphoreType.DMA((ticks,)),
            pltpu.SemaphoreType.DMA((ticks,)),
            pltpu.SemaphoreType.DMA((ticks, BATCHES)),
            pltpu.SemaphoreType.DMA((ticks, BATCHES)),
        ],
        compiler_params=pltpu.CompilerParams(
            collective_id=0, has_side_effects=True, vmem_limit_bytes=40 << 20
        ),
    )(motion, first, blocks, weight)
    return jnp.transpose(out, (0, 2, 1, 3))[None]


def solution(mesh):
    placed = (P("frame", None, None, "tile", None), P("frame", None, "tile", None), P(), P(), P())
    body = functools.partial(
        per_device, tiles=mesh.shape["tile"], sections=mesh.shape["frame"]
    )
    return jax.shard_map(
        body,
        mesh=mesh,
        in_specs=placed,
        out_specs=P("frame", None, None, "tile", None),
        check_vma=False,
    )
```

profile of v0, /device:TPU:1, one launch (start us, length us, event | category | flops | bytes accessed | tf_op | source)
XLA Modules:
  0.0 127.9 jit_solution(11270788774522302259)
XLA Ops:
  0.0 0.0 copy-start.3
  0.0 1.0 fusion.1
  1.0 0.1 copy.23
  1.1 0.2 copy.18
  1.3 0.2 stack.17
  1.5 0.1 copy.24
  1.6 0.2 copy.20
  1.8 0.2 stack.18
  2.0 0.0 copy-done.3
  2.0 0.0 copy-start.2
  2.0 0.2 fusion
  2.2 0.0 copy-start.1
  2.2 0.1 copy.15
  2.3 0.2 stack.15
  2.5 0.1 copy.16
  2.6 0.2 stack.16
  2.7 0.1 pad_maximum_fusion.weight_ref
  2.8 0.1 copy-done.2
  2.9 0.0 copy-start
  2.9 0.2 copy.21.motion_ref
  3.1 0.1 copy-done.1
  3.3 0.1 reshape_squeeze.9
  3.4 0.2 copy.13
  3.6 0.7 copy-done
  4.4 0.6 copy.26
  4.9 120.9 %shard_map.55 = bf16[3,16,64,256]{3,2,1,0:T(8,128)(2,1)S(1)} custom-call(s32[3,32,3,256]{3,2,1,0:T(4,128)S(1)} %copy.21.motion_ref, bf16[16,16,8,128]{3,2,1,0:T(8,128)(2,1)S(1)} %bitcast.22, bf16[3,16,64,256]{3,2,1,0:T(8,128)(2,1)S(1)} %bitcast.21, bf16[4,192,192]{2,1,0:T(8,128)(2,1)S(1)} %pad_maximum_fusion.weight_ref), custom_call_target="tpu_custom_call" | custom-call | tf_op jit(solution)/shard_map/pallas_call | solution.py:240
  125.9 2.0 %copy.22 = bf16[1,3,64,16,256]{4,3,2,1,0:T(8,128)(2,1)} copy(bf16[1,3,64,16,256]{4,2,3,1,0:T(8,128)(2,1)S(1)} %bitcast.20) | data formatting | bytes 3145728 | tf_op jit(solution)/shard_map/broadcast_in_dim | solution.py:264
  (1 shorter events, 0.0 us)
Async XLA Ops:
  0.0 2.0 %copy-start.3 = (bf16[64,1152]{1,0:T(8,128)(2,1)S(1)}, bf16[64,1152]{1,0:T(8,128)(2,1)}, u32[]{:S(2)}) copy-start(bf16[64,1152]{1,0:T(8,128)(2,1)} %param.8) | copy-start | bytes 442372
  2.0 1.0 copy-start.2
  2.2 1.1 copy-start.1
  2.9 1.4 %copy-start = (bf16[1,3,64,16,256]{4,3,2,1,0:T(8,128)(2,1)S(1)}, bf16[1,3,64,16,256]{4,3,2,1,0:T(8,128)(2,1)}, u32[]{:S(2)}) copy-start(bf16[1,3,64,16,256]{4,3,2,1,0:T(8,128)(2,1)} %param.5) | copy-start | bytes 4718596
where the time goes:
time: 128 us
  Pallas kernels  121 us (95%)
  local copies, waits for them, and re-layouts  6.78 us (5%)
    pallas_call x1, Pallas kernels, per_device(): pl.pallas_call(functools.partial(kernel, tiles, sections, ticks), out_sha...  121 us

commit v1 on v0

v1 whole, which is shorter than its diff:
```python
import functools

import jax
import jax.numpy as jnp
from jax import lax
from jax.experimental import pallas as pl
from jax.experimental.pallas import tpu as pltpu
from jax.sharding import PartitionSpec as P

BW = 32
MESH = pl.DeviceIdType.MESH
F32, BF16 = jnp.float32, jnp.bfloat16
BATCHES = 4
TOGETHER = 4


def row_taps(halves, lane):
    low, high = halves
    down_low, down_high = pltpu.roll(low, BW, 1), pltpu.roll(high, BW, 1)
    up_low, up_high = pltpu.roll(low, 128 - BW, 1), pltpu.roll(high, 128 - BW, 1)
    first, last = lane < BW, lane >= 128 - BW
    zero = jnp.zeros_like(low)
    left = jnp.concatenate(
        [jnp.where(first, zero, down_low), low, jnp.where(last, up_high, up_low)], axis=0
    )
    right = jnp.concatenate(
        [jnp.where(first, down_low, down_high), high, jnp.where(last, zero, up_high)], axis=0
    )
    return jnp.concatenate([left, right], axis=1)


def column_sum(product, width, col):
    halves = []
    for half in range(2):
        part = product[:, 128 * half : 128 * half + 128]
        before = jnp.where(col > 0, pltpu.roll(part[:width], 1, 1), 0.0)
        after = jnp.where(col < BW - 1, pltpu.roll(part[2 * width :], 127, 1), 0.0)
        halves.append(before + part[width : 2 * width] + after)
    return halves


def kernel(
    tiles, sections, ticks, motion_ref, first_ref, frames_ref, merge_ref, weight_ref, out_ref,
    moves, pieces, held_0, held_1, held_2, picked, arrived, part,
    moves_sem, one_send, one_recv, two_send, two_recv,
):
    held = (held_0, held_1, held_2)
    section = lax.axis_index("frame")
    owner = lax.axis_index("tile")
    ahead = lax.rem(section + 1, sections)
    behind = lax.rem(section + sections - 1, sections)
    per_owner = pieces.shape[2]
    width = out_ref.shape[2]
    span = per_owner // BATCHES

    moves_copy = pltpu.make_async_copy(motion_ref.at[:, section], moves, moves_sem)
    moves_copy.start()

    barrier = pltpu.get_barrier_semaphore()

    @pl.loop(1, tiles)
    def _(step):
        pl.semaphore_signal(
            barrier, inc=1, device_id={"tile": lax.rem(owner + step, tiles)}, device_id_type=MESH
        )

    @pl.loop(0, tiles)
    def _(step):
        pl.semaphore_signal(
            barrier, inc=1, device_id={"frame": behind, "tile": step}, device_id_type=MESH
        )

    pl.semaphore_wait(barrier, 2 * tiles - 1)

    order = sorted(range(1, tiles), key=lambda step: -min(step, tiles - step))

    def other_at(step):
        return lax.rem(owner + step, tiles)

    lane = lax.broadcasted_iota(jnp.int32, (width, 128), 1)
    col = lax.rem(lane, BW)

    mine = pl.ds(owner * per_owner, per_owner)
    for step in order:
        other = other_at(step)
        pltpu.make_async_remote_copy(
            src_ref=first_ref.at[other], dst_ref=held[0].at[mine],
            send_sem=one_send.at[0], recv_sem=one_recv.at[0],
            device_id={"tile": other}, device_id_type=MESH,
        ).start()
    held[0][mine] = first_ref[owner]

    def frame_taps(turn, carry):
        for tick in range(ticks):
            value = frames_ref[tick, turn]
            part[tick, turn] = row_taps((value[:, :128], value[:, 128:]), lane)
        return carry

    lax.fori_loop(0, per_owner, frame_taps, 0)

    for tick in range(ticks):
        if tick == 0:
            moves_copy.wait()
        landed = held[tick].at[pl.ds(0, (tiles - (tick == 0)) * per_owner)]
        pltpu.make_async_copy(landed, landed, one_recv.at[tick]).wait()

        for batch in range(BATCHES):
            group = pl.ds(batch * span, span)
            for step in order + [0]:
                other = other_at(step)
                for slot in range(batch * span, batch * span + span):
                    value = held[tick][moves[0, tick, other * per_owner + slot]]
                    if step:
                        picked[tick, other, slot] = value
                    else:
                        arrived[tick, owner, slot] = value
                if step:
                    pltpu.make_async_remote_copy(
                        src_ref=picked.at[tick, other, group],
                        dst_ref=arrived.at[tick, owner, group],
                        send_sem=two_send.at[tick, batch], recv_sem=two_recv.at[tick, batch],
                        device_id={"tile": other}, device_id_type=MESH,
                    ).start()

        for batch in range(BATCHES):
            group = pl.ds(batch * span, span)
            landed = arrived.at[tick, pl.ds(0, tiles - 1), group]
            pltpu.make_async_copy(landed, landed, two_recv.at[tick, batch]).wait()

            def some_blocks(turn, carry, tick=tick, batch=batch):
                blocks = [batch * span + turn * TOGETHER + local for local in range(TOGETHER)]

                def displaced(block):
                    down_by = moves[1, tick, owner * per_owner + block]
                    right_by = moves[2, tick, owner * per_owner + block]
                    offset = down_by * BW + right_by
                    col_at = col + right_by
                    turned = [
                        pltpu.roll(
                            jnp.concatenate(
                                [
                                    arrived[tick, 2 * i + j, block].astype(F32)
                                    for i in range(width // 8)
                                ],
                                axis=0,
                            ),
                            lax.rem(3 * 128 - offset, 128),
                            1,
                        ).astype(BF16)
                        for j in range(2)
                    ]
                    halves = []
                    for j in range(2):
                        source = lane + (128 * j + offset)
                        column = (col_at >= 0) & (col_at < BW)
                        from_low = column & (source >= 0) & (source < 128)
                        from_high = column & (source >= 128) & (source < 256)
                        rest = jnp.where(from_high, turned[1], jnp.zeros_like(turned[1]))
                        halves.append(jnp.where(from_low, turned[0], rest))
                    return halves

                def convolved(index, halves):
                    return jnp.dot(
                        weight_ref[index], row_taps(halves, lane), preferred_element_type=F32
                    )

                def merging(block, halves):
                    return jnp.dot(
                        merge_ref[...],
                        jnp.concatenate([part[tick, block], row_taps(halves, lane)], axis=0),
                        preferred_element_type=F32,
                    )

                values = [displaced(block) for block in blocks]
                merged = [
                    [
                        jnp.where(half > 0, half, 0.1 * half).astype(BF16)
                        for half in column_sum(merging(block, halves), width, col)
                    ]
                    for block, halves in zip(blocks, values)
                ]
                middle = [
                    [
                        jnp.maximum(half, 0.0).astype(BF16)
                        for half in column_sum(convolved(0, halves), width, col)
                    ]
                    for halves in merged
                ]
                for block, before, halves in zip(blocks, merged, middle):
                    added = column_sum(convolved(1, halves), width, col)
                    for j in range(2):
                        hidden = before[j].astype(F32) + added[j]
                        out_ref[tick, block, :, 128 * j : 128 * j + 128] = hidden.astype(BF16)
                        if tick + 1 < ticks:
                            for i in range(width // 8):
                                pieces[tick, 2 * i + j, block] = hidden[
                                    8 * i : 8 * i + 8
                                ].astype(BF16)
                return carry

            lax.fori_loop(0, span // TOGETHER, some_blocks, 0)

            if tick + 1 < ticks:
                for step in order + [0]:
                    other = other_at(step)
                    pltpu.make_async_remote_copy(
                        src_ref=pieces.at[tick, other, group],
                        dst_ref=held[tick + 1].at[
                            pl.ds(owner * per_owner + batch * span, span)
                        ],
                        send_sem=one_send.at[tick + 1],
                        recv_sem=one_recv.at[tick + 1],
                        device_id={"frame": ahead, "tile": other},
                        device_id_type=MESH,
                    ).start()

    sent = first_ref.at[pl.ds(0, tiles - 1)]
    pltpu.make_async_copy(sent, sent, one_send.at[0]).wait()
    for tick in range(ticks):
        if tick + 1 < ticks:
            sent = pieces.at[tick]
            pltpu.make_async_copy(sent, sent, one_send.at[tick + 1]).wait()
        for batch in range(BATCHES):
            sent = picked.at[tick, pl.ds(0, tiles - 1), pl.ds(batch * span, span)]
            pltpu.make_async_copy(sent, sent, two_send.at[tick, batch]).wait()


def stacked_weight(weight):
    out_width, columns = weight.shape
    taps = weight.reshape(out_width, 3, 3, columns // 9)
    return jnp.transpose(taps, (2, 0, 1, 3))


def per_device(frames, state_in, motion, merge_w, res_w, tiles, sections):
    ticks, width, per_owner, pixels = frames.shape[1:]
    first = state_in[0].reshape(width // 8, 8, per_owner, 2, 128)
    first = jnp.transpose(first, (0, 3, 2, 1, 4)).reshape(tiles, per_owner, 8, 128)
    blocks = jnp.transpose(frames[0], (0, 2, 1, 3))
    merge = stacked_weight(merge_w).reshape(3 * width, 3, 2, width)
    merge = jnp.transpose(merge, (0, 2, 1, 3)).reshape(3 * width, 6 * width)
    weight = jnp.stack([stacked_weight(res_w[0, 0]), stacked_weight(res_w[0, 1])])
    weight = weight.reshape(2, 3 * width, 3 * width)
    vmem = pl.BlockSpec(memory_space=pltpu.VMEM)
    piece = (per_owner, 8, 128)
    out = pl.pallas_call(
        functools.partial(kernel, tiles, sections, ticks),
        out_shape=jax.ShapeDtypeStruct((ticks, per_owner, width, pixels), BF16),
        in_specs=[pl.BlockSpec(memory_space=pl.ANY), vmem, vmem, vmem, vmem],
        out_specs=vmem,
        scratch_shapes=[
            pltpu.SMEM((3, ticks, tiles * per_owner), jnp.int32),
            pltpu.VMEM((ticks - 1, tiles) + piece, BF16),
            pltpu.VMEM((tiles * per_owner, 8, 128), BF16),
            pltpu.VMEM((tiles * per_owner, 8, 128), BF16),
            pltpu.VMEM((tiles * per_owner, 8, 128), BF16),
            pltpu.VMEM((ticks, tiles) + piece, BF16),
            pltpu.VMEM((ticks, tiles) + piece, BF16),
            pltpu.VMEM((ticks, per_owner, 3 * width, pixels), BF16),
            pltpu.SemaphoreType.DMA(()),
            pltpu.SemaphoreType.DMA((ticks,)),
            pltpu.SemaphoreType.DMA((ticks,)),
            pltpu.SemaphoreType.DMA((ticks, BATCHES)),
            pltpu.SemaphoreType.DMA((ticks, BATCHES)),
        ],
        compiler_params=pltpu.CompilerParams(
            collective_id=0, has_side_effects=True, vmem_limit_bytes=40 << 20
        ),
    )(motion, first, blocks, merge, weight)
    return jnp.transpose(out, (0, 2, 1, 3))[None]


def solution(mesh):
    placed = (P("frame", None, None, "tile", None), P("frame", None, "tile", None), P(), P(), P())
    body = functools.partial(
        per_device, tiles=mesh.shape["tile"], sections=mesh.shape["frame"]
    )
    return jax.shard_map(
        body,
        mesh=mesh,
        in_specs=placed,
        out_specs=P("frame", None, None, "tile", None),
        check_vma=False,
    )
```

time: 128 us -> 105 us (0.82)
  Pallas kernels: 121 us -> 98.1 us
    pallas_call x1, Pallas kernels: 121 us -> 98.1 us  [per_device(): pl.pallas_call(functools.partial(kernel, tiles, sections, ticks), out_sha...]
where the time goes in v1:
time: 105 us
  Pallas kernels  98.1 us (93%)
  local copies, waits for them, and re-layouts  6.32 us (6%)
    pallas_call x1, Pallas kernels, per_device(): pl.pallas_call(functools.partial(kernel, tiles, sections, ticks), out_sha...  98.1 us

profile of v1, /device:TPU:1, one launch (start us, length us, event | category | flops | bytes accessed | tf_op | source)
XLA Modules:
  0.0 104.6 jit_solution(7599667442815450596)
XLA Ops:
  0.0 0.0 copy-start.3
  0.0 1.0 fusion
  1.0 0.1 copy.23
  1.1 0.2 copy.17
  1.3 0.2 stack.9
  1.5 0.0 copy-start.2
  1.5 0.1 copy.24
  1.6 0.2 copy.19
  1.8 0.2 stack.10
  2.0 0.0 copy-start.1
  2.0 0.0 copy-done.3
  2.1 0.1 reshape.19
  2.3 0.2 copy.15
  2.4 0.0 copy-start
  2.5 0.1 copy.21.merge_ref
  2.6 0.0 copy-done.2
  2.6 0.2 copy.20.motion_ref
  2.8 0.2 copy-done.1
  3.0 0.1 reshape_squeeze.9
  3.2 0.2 copy.12
  3.4 0.5 copy-done
  3.9 0.6 copy.26
  4.5 98.1 %shard_map.55 = bf16[3,16,64,256]{3,2,1,0:T(8,128)(2,1)S(1)} custom-call(s32[3,32,3,256]{3,2,1,0:T(4,128)S(1)} %copy.20.motion_ref, bf16[16,16,8,128]{3,2,1,0:T(8,128)(2,1)S(1)} %bitcast.28, bf16[3,16,64,256]{3,2,1,0:T(8,128)(2,1)S(1)} %bitcast.27, bf16[192,384]{1,0:T(8,128)(2,1)S(1)} %copy.21.merge_ref, bf16[2,192,192]{2,1,0:T(8,128)(2,1)S(1)} %pad_maximum_fusion.weight_ref), custom_call_target="tpu_custom_call" | custom-call | tf_op jit(solution)/shard_map/pallas_call | solution.py:245
  102.5 2.0 %copy.22 = bf16[1,3,64,16,256]{4,3,2,1,0:T(8,128)(2,1)} copy(bf16[1,3,64,16,256]{4,2,3,1,0:T(8,128)(2,1)S(1)} %bitcast.26) | data formatting | bytes 3145728 | tf_op jit(solution)/shard_map/broadcast_in_dim | solution.py:269
  (3 shorter events, 0.1 us)
Async XLA Ops:
  0.0 2.0 %copy-start.3 = (bf16[64,1152]{1,0:T(8,128)(2,1)S(1)}, bf16[64,1152]{1,0:T(8,128)(2,1)}, u32[]{:S(2)}) copy-start(bf16[64,1152]{1,0:T(8,128)(2,1)} %param.8) | copy-start | bytes 442372
  1.5 1.1 %copy-start.2 = (s32[3,32,3,256]{3,1,2,0:T(8,128)S(1)}, s32[3,32,3,256]{3,1,2,0:T(8,128)}, u32[]{:S(2)}) copy-start(s32[3,32,3,256]{3,1,2,0:T(8,128)} %param.7) | copy-start | bytes 884740
  2.0 1.1 %copy-start.1 = (bf16[1,64,16,256]{3,2,1,0:T(8,128)(2,1)S(1)}, bf16[1,64,16,256]{3,2,1,0:T(8,128)(2,1)}, u32[]{:S(2)}) copy-start(bf16[1,64,16,256]{3,2,1,0:T(8,128)(2,1)} %param.6) | copy-start | bytes 1572868
  2.4 1.4 %copy-start = (bf16[1,3,64,16,256]{4,3,2,1,0:T(8,128)(2,1)S(1)}, bf16[1,3,64,16,256]{4,3,2,1,0:T(8,128)(2,1)}, u32[]{:S(2)}) copy-start(bf16[1,3,64,16,256]{4,3,2,1,0:T(8,128)(2,1)} %param.5) | copy-start | bytes 4718596

commit v2 on v1

--- a/solution.py
+++ b/solution.py
@@ -40,9 +40,9 @@
 
 
 def kernel(
-    tiles, sections, ticks, motion_ref, first_ref, frames_ref, merge_ref, weight_ref, out_ref,
-    moves, pieces, held_0, held_1, held_2, picked, arrived, part,
-    moves_sem, one_send, one_recv, two_send, two_recv,
+    tiles, sections, ticks, motion_ref, first_ref, frames_ref, merge_w_ref, res_w_ref, out_ref,
+    moves, turned_moves, merge_ref, weight_ref, pieces, held_0, held_1, held_2, picked, arrived, part,
+    moves_sem, turned_sem, one_send, one_recv, two_send, two_recv,
 ):
     held = (held_0, held_1, held_2)
     section = lax.axis_index("frame")
@@ -55,6 +55,10 @@
 
     moves_copy = pltpu.make_async_copy(motion_ref.at[:, section], moves, moves_sem)
     moves_copy.start()
+    odd = lax.rem(owner, 2)
+    turned = lax.rem(section + odd, sections)
+    turned_copy = pltpu.make_async_copy(motion_ref.at[:, turned], turned_moves, turned_sem)
+    turned_copy.start()
 
     barrier = pltpu.get_barrier_semaphore()
 
@@ -90,6 +94,22 @@
         ).start()
     held[0][mine] = first_ref[owner]
 
+    for right in range(3):
+        rows = pl.ds(right * width, width)
+        for down in range(3):
+            tap = 3 * down + right
+            merge_ref[rows, pl.ds(2 * width * down, 2 * width)] = merge_w_ref[
+                :, pl.ds(2 * width * tap, 2 * width)
+            ]
+        for layer in range(2):
+            weight_ref[layer, rows] = jnp.concatenate(
+                [
+                    res_w_ref[0, layer, :, pl.ds(width * (3 * down + right), width)]
+                    for down in range(3)
+                ],
+                axis=1,
+            )
+
     def frame_taps(turn, carry):
         for tick in range(ticks):
             value = frames_ref[tick, turn]
@@ -101,30 +121,46 @@
     for tick in range(ticks):
         if tick == 0:
             moves_copy.wait()
+            turned_copy.wait()
         landed = held[tick].at[pl.ds(0, (tiles - (tick == 0)) * per_owner)]
         pltpu.make_async_copy(landed, landed, one_recv.at[tick]).wait()
 
+        source_of = turned_moves if tick else moves
         for batch in range(BATCHES):
             group = pl.ds(batch * span, span)
             for step in order + [0]:
                 other = other_at(step)
                 for slot in range(batch * span, batch * span + span):
-                    value = held[tick][moves[0, tick, other * per_owner + slot]]
-                    if step:
-                        picked[tick, other, slot] = value
-                    else:
-                        arrived[tick, owner, slot] = value
-                if step:
+                    picked[tick, other, slot] = held[tick][
+                        source_of[0, tick, other * per_owner + slot]
+                    ]
+
+                def send(other=other, tick=tick, batch=batch, group=group):
                     pltpu.make_async_remote_copy(
                         src_ref=picked.at[tick, other, group],
                         dst_ref=arrived.at[tick, owner, group],
                         send_sem=two_send.at[tick, batch], recv_sem=two_recv.at[tick, batch],
-                        device_id={"tile": other}, device_id_type=MESH,
+                        device_id={"frame": turned if tick else section, "tile": other},
+                        device_id_type=MESH,
                     ).start()
+
+                def keep(tick=tick, batch=batch, group=group):
+                    pltpu.make_async_copy(
+                        picked.at[tick, owner, group], arrived.at[tick, owner, group],
+                        two_recv.at[tick, batch],
+                    ).start()
+
+                if step:
+                    send()
+                elif tick:
+                    pl.when(odd == 1)(send)
+                    pl.when(odd == 0)(keep)
+                else:
+                    keep()
 
         for batch in range(BATCHES):
             group = pl.ds(batch * span, span)
-            landed = arrived.at[tick, pl.ds(0, tiles - 1), group]
+            landed = arrived.at[tick, :, group]
             pltpu.make_async_copy(landed, landed, two_recv.at[tick, batch]).wait()
 
             def some_blocks(turn, carry, tick=tick, batch=batch):
@@ -165,9 +201,17 @@
                     )
 
                 def merging(block, halves):
+                    moved = row_taps(halves, lane)
                     return jnp.dot(
                         merge_ref[...],
-                        jnp.concatenate([part[tick, block], row_taps(halves, lane)], axis=0),
+                        jnp.concatenate(
+                            [
+                                taps[width * down : width * (down + 1)]
+                                for down in range(3)
+                                for taps in (part[tick, block], moved)
+                            ],
+                            axis=0,
+                        ),
                         preferred_element_type=F32,
                     )
 
@@ -203,32 +247,53 @@
             if tick + 1 < ticks:
                 for step in order + [0]:
                     other = other_at(step)
-                    pltpu.make_async_remote_copy(
-                        src_ref=pieces.at[tick, other, group],
-                        dst_ref=held[tick + 1].at[
-                            pl.ds(owner * per_owner + batch * span, span)
-                        ],
-                        send_sem=one_send.at[tick + 1],
-                        recv_sem=one_recv.at[tick + 1],
-                        device_id={"frame": ahead, "tile": other},
-                        device_id_type=MESH,
-                    ).start()
-
-    sent = first_ref.at[pl.ds(0, tiles - 1)]
-    pltpu.make_async_copy(sent, sent, one_send.at[0]).wait()
+                    target = pl.ds(owner * per_owner + batch * span, span)
+
+                    def send(other=other, tick=tick, group=group, target=target):
+                        pltpu.make_async_remote_copy(
+                            src_ref=pieces.at[tick, other, group],
+                            dst_ref=held[tick + 1].at[target],
+                            send_sem=one_send.at[tick + 1],
+                            recv_sem=one_recv.at[tick + 1],
+                            device_id={
+                                "frame": lax.rem(section + 1 - lax.rem(other, 2), sections),
+                                "tile": other,
+                            },
+                            device_id_type=MESH,
+                        ).start()
+
+                    def keep(tick=tick, group=group, target=target):
+                        pltpu.make_async_copy(
+                            pieces.at[tick, owner, group], held[tick + 1].at[target],
+                            one_recv.at[tick + 1],
+                        ).start()
+
+                    if step:
+                        send()
+                    else:
+                        pl.when(odd == 0)(send)
+                        pl.when(odd == 1)(keep)
+
+    def drained(source, count, sem, *rest):
+        sent = source.at[(*rest[:1], pl.ds(0, count), *rest[1:])]
+        pltpu.make_async_copy(sent, sent, sem).wait()
+
+    drained(first_ref, tiles - 1, one_send.at[0])
     for tick in range(ticks):
+        for batch in range(BATCHES):
+            group = pl.ds(batch * span, span)
+            if tick == 0:
+                drained(picked, tiles - 1, two_send.at[tick, batch], tick, group)
+                continue
+            for parity, count in ((0, tiles - 1), (1, tiles)):
+                @pl.when(odd == parity)
+                def _(tick=tick, batch=batch, group=group, count=count):
+                    drained(picked, count, two_send.at[tick, batch], tick, group)
         if tick + 1 < ticks:
-            sent = pieces.at[tick]
-            pltpu.make_async_copy(sent, sent, one_send.at[tick + 1]).wait()
-        for batch in range(BATCHES):
-            sent = picked.at[tick, pl.ds(0, tiles - 1), pl.ds(batch * span, span)]
-            pltpu.make_async_copy(sent, sent, two_send.at[tick, batch]).wait()
-
-
-def stacked_weight(weight):
-    out_width, columns = weight.shape
-    taps = weight.reshape(out_width, 3, 3, columns // 9)
-    return jnp.transpose(taps, (2, 0, 1, 3))
+            for parity, count in ((0, tiles), (1, tiles - 1)):
+                @pl.when(odd == parity)
+                def _(tick=tick, count=count):
+                    drained(pieces, count, one_send.at[tick + 1], tick)
 
 
 def per_device(frames, state_in, motion, merge_w, res_w, tiles, sections):
@@ -236,10 +301,6 @@
     first = state_in[0].reshape(width // 8, 8, per_owner, 2, 128)
     first = jnp.transpose(first, (0, 3, 2, 1, 4)).reshape(tiles, per_owner, 8, 128)
     blocks = jnp.transpose(frames[0], (0, 2, 1, 3))
-    merge = stacked_weight(merge_w).reshape(3 * width, 3, 2, width)
-    merge = jnp.transpose(merge, (0, 2, 1, 3)).reshape(3 * width, 6 * width)
-    weight = jnp.stack([stacked_weight(res_w[0, 0]), stacked_weight(res_w[0, 1])])
-    weight = weight.reshape(2, 3 * width, 3 * width)
     vmem = pl.BlockSpec(memory_space=pltpu.VMEM)
     piece = (per_owner, 8, 128)
     out = pl.pallas_call(
@@ -249,6 +310,9 @@
         out_specs=vmem,
         scratch_shapes=[
             pltpu.SMEM((3, ticks, tiles * per_owner), jnp.int32),
+            pltpu.SMEM((3, ticks, tiles * per_owner), jnp.int32),
+            pltpu.VMEM((3 * width, 6 * width), BF16),
+            pltpu.VMEM((2, 3 * width, 3 * width), BF16),
             pltpu.VMEM((ticks - 1, tiles) + piece, BF16),
             pltpu.VMEM((tiles * per_owner, 8, 128), BF16),
             pltpu.VMEM((tiles * per_owner, 8, 128), BF16),
@@ -256,6 +320,7 @@
             pltpu.VMEM((ticks, tiles) + piece, BF16),
             pltpu.VMEM((ticks, tiles) + piece, BF16),
             pltpu.VMEM((ticks, per_owner, 3 * width, pixels), BF16),
+            pltpu.SemaphoreType.DMA(()),
             pltpu.SemaphoreType.DMA(()),
             pltpu.SemaphoreType.DMA((ticks,)),
             pltpu.SemaphoreType.DMA((ticks,)),
@@ -265,7 +330,7 @@
         compiler_params=pltpu.CompilerParams(
             collective_id=0, has_side_effects=True, vmem_limit_bytes=40 << 20
         ),
-    )(motion, first, blocks, merge, weight)
+    )(motion, first, blocks, merge_w, res_w)
     return jnp.transpose(out, (0, 2, 1, 3))[None]
 
 

time: 105 us -> 102 us (0.971)
  Pallas kernels: 98.1 us -> 96.4 us
    pallas_call x1, Pallas kernels: 98.1 us -> 96.4 us  [per_device(): pl.pallas_call(functools.partial(kernel, tiles, sections, ticks), out_sha...]
    unnamed x12 -> x8, local copies, waits for them, and re-layouts: 1.79 us -> 2.26 us
where the time goes in v2:
time: 102 us
  Pallas kernels  96.4 us (95%)
  local copies, waits for them, and re-layouts  5.66 us (6%)
    pallas_call x1, Pallas kernels, per_device(): pl.pallas_call(functools.partial(kernel, tiles, sections, ticks), out_sha...  96.4 us
    unnamed x8, local copies, waits for them, and re-layouts  2.26 us

profile of v2, /device:TPU:1, one launch (start us, length us, event | category | flops | bytes accessed | tf_op | source)
XLA Modules:
  0.0 102.1 jit_solution(12343827968242965151)
XLA Ops:
  0.0 0.0 copy-start.2
  0.0 1.3 %copy.8.motion_ref = s32[3,32,3,256]{3,2,1,0:T(4,128)S(1)} copy(s32[3,32,3,256]{3,1,2,0:T(8,128)} %param.7) | data formatting | bytes 589824 | tf_op args[2]
  1.3 1.2 %reshape_squeeze.3 = bf16[8,8,16,2,128]{4,3,2,1,0:T(2,128)(2,1)S(1)} reshape(bf16[1,64,16,256]{3,2,1,0:T(8,128)(2,1)} %param.6) | data formatting | bytes 1048576 | tf_op jit(solution)/shard_map/reshape;squeeze | solution.py:301
  2.5 0.2 copy.6
  2.7 0.0 copy-done.2
  2.7 0.0 copy-start
  2.7 0.0 copy-start.1
  2.7 0.6 copy.11
  3.3 0.3 copy-done
  3.6 0.1 copy-done.1
  3.7 96.4 %shard_map.55 = bf16[3,16,64,256]{3,2,1,0:T(8,128)(2,1)S(1)} custom-call(s32[3,32,3,256]{3,2,1,0:T(4,128)S(1)} %copy.8.motion_ref, bf16[16,16,8,128]{3,2,1,0:T(8,128)(2,1)S(1)} %bitcast.15, bf16[3,16,64,256]{3,2,1,0:T(8,128)(2,1)S(1)} %bitcast.14, bf16[64,1152]{1,0:T(8,128)(2,1)S(1)} %copy-done.1, bf16[1,2,64,576]{3,2,1,0:T(8,128)(2,1)S(1)} %copy-done), custom_call_target="tpu_custom_call" | custom-call | tf_op jit(solution)/shard_map/pallas_call | solution.py:306
  100.1 2.0 %copy.9 = bf16[1,3,64,16,256]{4,3,2,1,0:T(8,128)(2,1)} copy(bf16[1,3,64,16,256]{4,2,3,1,0:T(8,128)(2,1)S(1)} %bitcast.13) | data formatting | bytes 3145728 | tf_op jit(solution)/shard_map/broadcast_in_dim | solution.py:334
Async XLA Ops:
  0.0 2.7 %copy-start.2 = (bf16[1,3,64,16,256]{4,3,2,1,0:T(8,128)(2,1)S(1)}, bf16[1,3,64,16,256]{4,3,2,1,0:T(8,128)(2,1)}, u32[]{:S(2)}) copy-start(bf16[1,3,64,16,256]{4,3,2,1,0:T(8,128)(2,1)} %param.5) | copy-start | bytes 4718596
  2.7 0.9 copy-start
  2.7 1.0 copy-start.1
